TPU v7x, 128 devices: a whole 4x4x4 slice. The times are simulated.
128 devices in a mesh: blk: 8 (over z, core), grp: 16 (over x, y).
Axes of the slice: x: 4, y: 4, z: 4, core: 2. Of those that a mesh axis runs over, the one named last changes fastest.
Arguments:
- user_prior: float32 [32768, 128], P(('blk', 'grp')), may hold values from -6 to 6
- item_factors: bfloat16 [524288, 128], P(('blk', 'grp')), may hold values from -0.375 to 0.375
- user_tiles: int32 [8192], P(('blk', 'grp')), may hold values from 0 to 31
- item_tiles: int32 [8192], P(('blk', 'grp')), may hold values from 0 to 4095, as said below
- counts: int32 [8192, 128, 128], P(('blk', 'grp')), may hold values from 0 to 20, as said below
Outputs:
- user_factors: float32 [32768, 128], P(('blk', 'grp'))
Inputs may be any that keep to these rules, and one draw needn't show every extreme that they name: `item_tiles`: item tile t is held by device t // 32 of blk+grp. The entries of one device name tiles of 32 different holders, exactly 2 entries for each holder that they name, in no particular order. In each device's 64 entries, those whose tile of counts has a nonzero value come before those whose tile is all zero; in every group along grp at least one device has all 64 entries of the first kind.
All inputs are finite; a program needn't handle non-finite values.
Results may differ from a plain program's by a relative error of at most 0.0003.
The roundings to bfloat16 on the way count: a program that leaves them out, or rounds other values in their place, can miss the bound.
Values may be sent and summed in bfloat16 or wider, within the bound.
A program may use at most 128 MiB of HBM per device.

v0:
```python
import jax
import jax.numpy as jnp
from jax import lax
from jax.sharding import PartitionSpec as P

ITERS = 3
ALPHA = 40.0
REG = 32.0
EPS = 1e-06


def fetch_tiles(item_factors, item_tiles, pairs, tile, rank):
    n_all = lax.axis_size(("blk", "grp"))
    tiles_held = item_factors.shape[0] // tile
    slots_each = max(2, pairs // n_all)
    owner = item_tiles // tiles_held
    local_slot = item_tiles % tiles_held
    position = jnp.arange(pairs, dtype=jnp.int32)
    earlier = (owner[None, :] == owner[:, None]) & (position[None, :] < position[:, None])
    order = jnp.sum(earlier.astype(jnp.int32), axis=1)
    requests = jnp.full((n_all, slots_each), -1, jnp.int32).at[owner, order].set(local_slot)
    wanted = lax.all_to_all(requests, ("blk", "grp"), split_axis=0, concat_axis=0, tiled=True)
    held = item_factors.reshape(tiles_held, tile, rank)
    picked = jnp.take(held, jnp.maximum(wanted, 0), axis=0)
    picked = jnp.where((wanted >= 0)[:, :, None, None], picked, jnp.zeros((), picked.dtype))
    arrived = lax.all_to_all(picked, ("blk", "grp"), split_axis=0, concat_axis=0, tiled=True)
    return arrived[owner, order]


def body(user_prior, item_factors, user_tiles, item_tiles, counts):
    pairs = counts.shape[0]
    tile = counts.shape[1]
    rank = item_factors.shape[1]
    n_grp = lax.axis_size("grp")
    own_rows = user_prior.shape[0]
    block_rows = own_rows * n_grp
    user_blocks = block_rows // tile
    span = min(32, pairs)
    gram_local = lax.dot_general(
        item_factors, item_factors, (((0,), (0,)), ((), ())), preferred_element_type=jnp.float32
    )
    gram = lax.psum(gram_local, ("blk", "grp"))
    pair_tiles = fetch_tiles(item_factors, item_tiles, pairs, tile, rank)
    live = jnp.sum(jnp.any(counts > 0, axis=(1, 2)).astype(jnp.int32))
    rounds = (live + span - 1) // span
    tile_ids = jnp.arange(user_blocks, dtype=jnp.int32)

    def accumulate(low_tiles, with_rhs):

        def one_round(index, totals):
            start = index * span
            users = lax.dynamic_slice_in_dim(user_tiles, start, span)
            factors = lax.dynamic_slice_in_dim(pair_tiles, start, span)
            counted = lax.dynamic_slice_in_dim(counts, start, span).astype(jnp.float32)
            selector = (tile_ids[:, None] == users[None, :]).astype(jnp.float32)
            users_low = jnp.take(low_tiles, users, axis=0)
            scores = jnp.einsum(
                "bur,bir->bui", users_low, factors, preferred_element_type=jnp.float32
            )
            scaled = (ALPHA * counted * scores).astype(jnp.bfloat16)
            back = jnp.einsum("bui,bir->bur", scaled, factors, preferred_element_type=jnp.float32)
            result = [
                totals[0]
                + jnp.einsum("tb,bur->tur", selector, back, precision=lax.Precision.HIGHEST)
            ]
            if with_rhs:
                confidence = jnp.where(counted > 0, 1.0 + ALPHA * counted, 0.0).astype(jnp.bfloat16)
                pulled = jnp.einsum(
                    "bui,bir->bur", confidence, factors, preferred_element_type=jnp.float32
                )
                result.append(
                    totals[1]
                    + jnp.einsum("tb,bur->tur", selector, pulled, precision=lax.Precision.HIGHEST)
                )
            return tuple(result)

        zeros = jnp.zeros((user_blocks, tile, rank), jnp.float32)
        start_state = (zeros, zeros) if with_rhs else (zeros,)
        totals = lax.fori_loop(0, rounds, one_round, start_state)
        return tuple((total.reshape(block_rows, rank) for total in totals))

    def gram_term(vectors):
        return jnp.dot(vectors, gram, precision=lax.Precision.HIGHEST) + REG * vectors

    def row_sum(left, right):
        return jnp.sum(left * right, axis=1, keepdims=True)

    whole = lax.all_gather(user_prior, "grp", axis=0, tiled=True)
    pair_part, rhs_part = accumulate(
        whole.astype(jnp.bfloat16).reshape(user_blocks, tile, rank), True
    )
    pair_total, rhs_total = lax.psum((pair_part, rhs_part), "grp")
    solution = whole
    residual = rhs_total - (gram_term(solution) + pair_total)
    direction = residual
    norm_now = row_sum(residual, residual)
    for step in range(ITERS):
        (pair_part,) = accumulate(
            direction.astype(jnp.bfloat16).reshape(user_blocks, tile, rank), False
        )
        image = gram_term(direction) + lax.psum(pair_part, "grp")
        alpha = norm_now / (row_sum(direction, image) + EPS)
        solution = solution + alpha * direction
        residual = residual - alpha * image
        fresh = row_sum(residual, residual)
        direction = residual + fresh / (norm_now + EPS) * direction
        norm_now = fresh
    return lax.dynamic_slice_in_dim(solution, lax.axis_index("grp") * own_rows, own_rows, 0)


def solution(mesh):
    in_specs = (
        P(("blk", "grp"), None),
        P(("blk", "grp"), None),
        P(("blk", "grp")),
        P(("blk", "grp")),
        P(("blk", "grp"), None, None),
    )
    out_specs = P(("blk", "grp"), None)
    return jax.shard_map(body, mesh=mesh, in_specs=in_specs, out_specs=out_specs, check_vma=False)
```

profile of v0, /device:TPU:0, one launch (start us, length us, event | category | flops | bytes accessed | tf_op | source)
XLA Modules:
  0.0 787.2 jit_solution(2010041510047153230)
XLA Ops:
  15.4 20.5 %all_to_all.14 = s32[128,1,2]{2,1,0:T(1,128)S(1)} all-to-all(s32[128,1,2]{2,1,0:T(1,128)S(1)} %copy.108), channel_id=1, replica_groups=mesh['blk'=8,'grp'=16] {'blk','grp'}, dimensions={0} | all-to-all | bytes 2048 | tf_op jit(solution)/shard_map/all_to_all | solution.py:22
  36.5 8.4 %gather_fusion.4 = bf16[256,128,128]{2,1,0:T(8,128)(2,1)} fusion(bf16[32,128,128]{2,1,0:T(8,128)(2,1)S(1)} %bitcast.108, s32[1024]{0:T(1024)S(1)} %pad_clamp_fusion.4), kind=kCustom, calls=%fused_computation.4 | custom fusion | bytes 16778240 | tf_op jit(solution)/shard_map/jit(_take)/gather | solution.py:24
  44.9 7.4 select_select_fusion
  52.3 6.1 all-to-all-start.1
  61.1 104.8 %all-gather.2.cloned.1.call-done = f32[4096,128]{0,1:T(8,128)} async-done(((f32[256,128]{0,1:T(8,128)}), f32[4096,128]{0,1:T(8,128)}) %all-gather.2.cloned.1.call-update) | async-done | bytes 2097168 | tf_op jit(solution)/shard_map/all_gather | solution.py:88
  176.5 18.2 %while.46 = (s32[]{:T(128)}, f32[32,128,128]{2,0,1:T(8,128)}, f32[32,128,128]{2,0,1:T(8,128)}, s32[]{:T(128)}, s32[64]{0:T(128)S(1)}, /*index=5*/s32[64,128,128]...) while((s32[]{:T(128)}, f32[32,128,128]{2,0,1:T(8,128)}, ...), condition=%wide.region_5.7_spmd.clone, body=%wide.region_4.6_spmd.clone.sunk | while | flops 812125440 | bytes 44048128 | solution.py:79
  182.9 6.1 fusion.187
  189.4 5.4 fusion.189
  198.3 4.6 copy.165
  206.3 4.6 copy.166
  211.2 58.5 %all-reduce.7.cloned.1.call-done = f32[128,128]{1,0:T(8,128)} async-done(((f32[128,128]{1,0:T(8,128)}), f32[128,128]{1,0:T(8,128)}) %all-reduce.7.cloned.1.call-update) | async-done | bytes 65552 | tf_op jit(solution)/shard_map/psum | solution.py:42
  269.7 105.7 %all-reduce.15.cloned.1.call-done = (f32[4096,128]{0,1:T(8,128)}, f32[4096,128]{0,1:T(8,128)}) async-done(((f32[4096,128]{0,1:T(8,128)}, f32[4096,128]{0,1:T(8,128)}), (f32[4096,128]{0,1:T(8,128)}, f32[4096,128]{0,1:T(8,128)})) %all-reduce.15.cloned.1.call-update) | async-done | bytes 4194320 | tf_op jit(solution)/shard_map/psum | solution.py:92
  375.5 7.0 fusion.133
  385.4 12.0 %while.47 = (s32[]{:T(128)}, f32[32,128,128]{2,0,1:T(8,128)}, s32[]{:T(128)}, s32[64]{0:T(128)S(1)}, s32[64,128,128]{2,1,0:T(8,128)}, /*index=5*/bf16[32,128,128...) while((s32[]{:T(128)}, f32[32,128,128]{2,0,1:T(8,128)}, ...), condition=%wide.region_11.13_spmd.clone, body=%wide.region_10.12_spmd.clone.sunk | while | flops 472910112 | bytes 15735391 | solution.py:79
  391.5 5.9 fusion.196
  405.9 102.4 %all-reduce.9.cloned.1.call-done = f32[4096,128]{0,1:T(8,128)} async-done(((f32[4096,128]{0,1:T(8,128)}), f32[4096,128]{0,1:T(8,128)}) %all-reduce.9.cloned.1.call-update) | async-done | bytes 2097168 | tf_op jit(solution)/shard_map/psum | solution.py:101
  508.3 5.5 multiply_reduce_fusion.3
  519.1 12.1 %while.48 = (s32[]{:T(128)}, f32[32,128,128]{2,0,1:T(8,128)}, s32[]{:T(128)}, s32[64]{0:T(128)S(1)}, s32[64,128,128]{2,1,0:T(8,128)}, /*index=5*/bf16[32,128,128...) while((s32[]{:T(128)}, f32[32,128,128]{2,0,1:T(8,128)}, ...), condition=%wide.region_16.18_spmd.clone, body=%wide.region_15.17_spmd.clone.sunk | while | flops 472910112 | bytes 15735391 | solution.py:79
  525.3 5.9 fusion.203
  539.5 101.9 %all-reduce.11.cloned.1.call-done = f32[4096,128]{0,1:T(8,128)} async-done(((f32[4096,128]{0,1:T(8,128)}), f32[4096,128]{0,1:T(8,128)}) %all-reduce.11.cloned.1.call-update) | async-done | bytes 2097168 | tf_op jit(solution)/shard_map/psum | solution.py:101
  641.4 5.3 multiply_reduce_fusion.1
  653.1 12.3 %while.49 = (s32[]{:T(128)}, f32[32,128,128]{2,0,1:T(8,128)}, s32[]{:T(128)}, s32[64]{0:T(128)S(1)}, s32[64,128,128]{2,1,0:T(8,128)}, /*index=5*/bf16[32,128,128...) while((s32[]{:T(128)}, f32[32,128,128]{2,0,1:T(8,128)}, ...), condition=%wide.region_21.23_spmd.clone, body=%wide.region_20.22_spmd.clone.sunk | while | flops 472910112 | bytes 15735391 | solution.py:79
  659.3 5.9 fusion.210
  671.3 102.4 %all-reduce.13.cloned.1.call-done = f32[4096,128]{0,1:T(8,128)} async-done(((f32[4096,128]{0,1:T(8,128)}), f32[4096,128]{0,1:T(8,128)}) %all-reduce.13.cloned.1.call-update) | async-done | bytes 2097168 | tf_op jit(solution)/shard_map/psum | solution.py:101
  (109 shorter events, 96.5 us)
Async XLA Ops:
  7.4 29.1 %copy-start = (bf16[4096,128]{1,0:T(8,128)(2,1)S(1)}, bf16[4096,128]{1,0:T(8,128)(2,1)}, u32[]{:S(2)}) copy-start(bf16[4096,128]{1,0:T(8,128)(2,1)} %param.16) | copy-start | bytes 3145732
  7.4 3.5 copy-start.11
  52.3 6.1 copy-start.10
  52.3 116.7 %all-to-all-start.1 = ((bf16[128,2,128,128]{3,2,1,0:T(8,128)(2,1)}), bf16[128,2,128,128]{3,2,1,0:T(8,128)(2,1)}, u32[]{:S(2)}, u32[]{:S(2)}) async-start(bf16[128,2,128,128]{3,2,1,0:T(8,128)(2,1)} %select_select_fusion), calls=%async_computation.1 | async-start | bytes 16777216 | tf_op jit(solution)/shard_map/all_to_all | solution.py:26
  58.4 107.5 %all-gather.2.cloned.1.call-start = ((), (), s32[]{:S(2)}) async-start(), calls=%async_computation.2 | async-start | bytes 2228224 | tf_op jit(solution)/shard_map/all_gather | solution.py:88
  59.2 210.5 %all-reduce.7.cloned.1.call-start = ((), (), s32[]{:S(2)}) async-start(), calls=%async_computation.3 | async-start | bytes 131072 | tf_op jit(solution)/shard_map/psum | solution.py:42
  60.4 315.1 %all-reduce.15.cloned.1.call-start = ((), (), s32[]{:S(2)}) async-start(), calls=%async_computation.7 | async-start | bytes 8388608 | tf_op jit(solution)/shard_map/psum | solution.py:92
  173.3 3.2 copy-start.9
  182.9 6.1 copy-start.2
  210.9 297.3 %all-reduce.9.cloned.1.call-start = ((), (), s32[]{:S(2)}) async-start(), calls=%async_computation.4 | async-start | bytes 4194304 | tf_op jit(solution)/shard_map/psum | solution.py:101
  405.4 102.9 %copy-start.8 = (f32[128,128]{1,0:T(8,128)S(1)}, f32[128,128]{1,0:T(8,128)}, u32[]{:S(2)}) copy-start(f32[128,128]{1,0:T(8,128)} %all-reduce.7.cloned.1.call-done) | copy-start | bytes 196612
  405.4 236.0 %all-reduce.11.cloned.1.call-start = ((), (), s32[]{:S(2)}) async-start(), calls=%async_computation.5 | async-start | bytes 4194304 | tf_op jit(solution)/shard_map/psum | solution.py:101
  508.3 5.5 copy-start.3
  514.2 2.0 copy-start.4
  539.3 234.4 %all-reduce.13.cloned.1.call-start = ((), (), s32[]{:S(2)}) async-start(), calls=%async_computation.6 | async-start | bytes 4194304 | tf_op jit(solution)/shard_map/psum | solution.py:101
  641.4 5.4 copy-start.5
  646.7 1.6 copy-start.6
  671.1 102.6 %copy-start.7 = (f32[4096,128]{0,1:T(8,128)S(1)}, f32[4096,128]{0,1:T(8,128)}, u32[]{:S(2)}) copy-start(f32[4096,128]{0,1:T(8,128)} %get-tuple-element.504) | copy-start | bytes 6291460
  773.7 5.9 copy-start.1
Sparse Core Ops, SparseCore 0:
  61.3 104.5 all-gather.1
  405.5 102.6 all-reduce.8
  671.2 102.3 all-reduce.12
Sparse Core Ops, SparseCore 1:
  64.5 205.2 all-reduce.6
  273.0 102.4 all-reduce.14
  539.3 102.0 all-reduce.10
where the time goes:
time: 795 us; the launch traced here: 787 us
  waiting for transfers between devices  576 us (72%)
  local copies, waits for them, and re-layouts  78.9 us (10%)
  matrix products  69 us (9%)
  blocking collectives  20.5 us (3%)
  other arithmetic  19.5 us (2%)
  between operations  16 us (2%)
    psum x3, waiting for transfers between devices, body(): image = gram_term(direction) + lax.psum(pair_part, 'grp')  307 us
    psum x1, waiting for transfers between devices, body(): pair_total, rhs_total = lax.psum((pair_part, rhs_part), 'grp')  106 us
    all_gather x1, waiting for transfers between devices, body(): whole = lax.all_gather(user_prior, 'grp', axis=0, tiled=True)  105 us
    psum x1, waiting for transfers between devices, body(): gram = lax.psum(gram_local, ('blk', 'grp'))  58.5 us
    unnamed x32, local copies, waits for them, and re-layouts  28.6 us
    dot_general x4, matrix products, one_round(): jnp.einsum('tb,bur->tur', selector, back, precision=lax.Precision.HIGHEST)  23.8 us
    dot_general x4, matrix products, gram_term(): jnp.dot(vectors, gram, precision=lax.Precision.HIGHEST) + REG * vectors  21.8 us
    all_to_all x1, blocking collectives, fetch_tiles(): lax.all_to_all(requests, ('blk', 'grp'), split_axis=0, concat_axis=0, til...  20.5 us
  transfers between devices with their start and end apart: 7, of which 6 were waited for; matrix products, arithmetic and copies ran while one was open for 6% of the time, Pallas kernels for 0%

commit v1 on v0

--- a/solution.py
+++ b/solution.py
@@ -39,7 +39,7 @@
     gram_local = lax.dot_general(
         item_factors, item_factors, (((0,), (0,)), ((), ())), preferred_element_type=jnp.float32
     )
-    gram = lax.psum(gram_local, ("blk", "grp"))
+    gram = jnp.sum(lax.all_gather(gram_local, ("blk", "grp")), axis=0)
     pair_tiles = fetch_tiles(item_factors, item_tiles, pairs, tile, rank)
     live = jnp.sum(jnp.any(counts > 0, axis=(1, 2)).astype(jnp.int32))
     rounds = (live + span - 1) // span

time: 795 us -> 746 us (0.938)
  waiting for transfers between devices: 576 us -> 532 us
  blocking collectives: 20.5 us -> 0 us
  starting transfers between devices: 7.1 us -> 18.1 us
    all_gather x1, waiting for transfers between devices: 105 us -> 0.02 us  [body(): whole = lax.all_gather(user_prior, 'grp', axis=0, tiled=True)]
    all_to_all x1, waiting for transfers between devices: 0.01 us -> 96.6 us  [fetch_tiles(): lax.all_to_all(picked, ('blk', 'grp'), split_axis=0, concat_axis=0, tiled...]
    psum x1 -> x0, waiting for transfers between devices: 58.5 us -> none  [body(): gram = lax.psum(gram_local, ('blk', 'grp'))]
    all_to_all x1 -> x0, blocking collectives: 20.5 us -> none  [fetch_tiles(): lax.all_to_all(requests, ('blk', 'grp'), split_axis=0, concat_axis=0, til...]
    psum x1, waiting for transfers between devices: 106 us -> 119 us  [body(): pair_total, rhs_total = lax.psum((pair_part, rhs_part), 'grp')]
    all_to_all x0 -> x1, starting transfers between devices: none -> 11.2 us  [fetch_tiles(): lax.all_to_all(requests, ('blk', 'grp'), split_axis=0, concat_axis=0, til...]
    all_to_all x0 -> x1, waiting for transfers between devices: none -> 8.33 us  [fetch_tiles(): lax.all_to_all(requests, ('blk', 'grp'), split_axis=0, concat_axis=0, til...]
    unnamed x32 -> x26, local copies, waits for them, and re-layouts: 28.6 us -> 29.7 us
  transfers between devices with their start and end apart: 7 -> 8, of which waited for: 6 -> 6; matrix products, arithmetic and copies ran while one was open for 6% -> 10% of each run, Pallas kernels for 0% -> 0%
where the time goes in v1:
time: 746 us; the launch traced here: 739 us
  waiting for transfers between devices  532 us (71%)
  local copies, waits for them, and re-layouts  80.5 us (11%)
  matrix products  70.4 us (9%)
  other arithmetic  23.2 us (3%)
  starting transfers between devices  18.1 us (2%)
  between operations  14.5 us (2%)
    psum x3, waiting for transfers between devices, body(): image = gram_term(direction) + lax.psum(pair_part, 'grp')  307 us
    psum x1, waiting for transfers between devices, body(): pair_total, rhs_total = lax.psum((pair_part, rhs_part), 'grp')  119 us
    all_to_all x1, waiting for transfers between devices, fetch_tiles(): lax.all_to_all(picked, ('blk', 'grp'), split_axis=0, concat_axis=0, tiled...  96.6 us
    unnamed x26, local copies, waits for them, and re-layouts  29.7 us
    dot_general x4, matrix products, one_round(): jnp.einsum('tb,bur->tur', selector, back, precision=lax.Precision.HIGHEST)  23.8 us
    dot_general x4, matrix products, gram_term(): jnp.dot(vectors, gram, precision=lax.Precision.HIGHEST) + REG * vectors  23 us
    dot_general x4, matrix products, one_round(): jnp.einsum('bui,bir->bur', scaled, factors, preferred_element_type=jnp.fl...  16.4 us
    while x5, local copies, waits for them, and re-layouts, accumulate(): totals = lax.fori_loop(0, rounds, one_round, start_state)  16.4 us
  transfers between devices with their start and end apart: 8, of which 6 were waited for; matrix products, arithmetic and copies ran while one was open for 10% of the time, Pallas kernels for 0%

profile of v1, /device:TPU:0, one launch (start us, length us, event | category | flops | bytes accessed | tf_op | source)
XLA Modules:
  0.0 738.7 jit_solution(9707504253034539134)
XLA Ops:
  16.8 11.2 %all-to-all-start = ((s32[128,1,2]{2,1,0:T(1,128)}), s32[128,1,2]{2,1,0:T(1,128)S(1)}, u32[]{:S(2)}, u32[]{:S(2)}) async-start(s32[128,1,2]{2,1,0:T(1,128)} %copy.108), calls=%async_computation | async-start | bytes 131072 | tf_op jit(solution)/shard_map/all_to_all | solution.py:22
  29.2 8.3 %all-to-all-done = s32[128,1,2]{2,1,0:T(1,128)S(1)} async-done(((s32[128,1,2]{2,1,0:T(1,128)}), s32[128,1,2]{2,1,0:T(1,128)S(1)}, u32[]{:S(2)}, u32[]{:S(2)}) %all-to-all-start) | async-done | bytes 1056 | tf_op jit(solution)/shard_map/all_to_all | solution.py:22
  38.1 8.4 %gather_fusion.4 = bf16[256,128,128]{2,1,0:T(8,128)(2,1)} fusion(bf16[32,128,128]{2,1,0:T(8,128)(2,1)S(1)} %bitcast.109, s32[1024]{0:T(1024)S(1)} %pad_clamp_fusion.4), kind=kCustom, calls=%fused_computation.4 | custom fusion | bytes 16778240 | tf_op jit(solution)/shard_map/jit(_take)/gather | solution.py:24
  46.5 7.4 %select_select_fusion = bf16[128,2,128,128]{3,2,1,0:T(8,128)(2,1)} fusion(bf16[128,2,128,128]{3,2,1,0:T(8,128)(2,1)} %bitcast.115, pred[128,2]{1,0:T(8,128)(4,1)S(1)} %copy.112, pred[128,2]{1,0:T(8,128)(4,1)S(1)} %copy.110), kind=kLoop, calls=%fused_computation.103 | loop fusion | flops 8388608 | bytes 16777728 | tf_op jit(solution)/shard_map/jit(_where)/select_n | solution.py:25
  53.9 5.9 all-to-all-start.1
  63.6 96.6 %all-to-all-done.1 = bf16[128,2,128,128]{3,2,1,0:T(8,128)(2,1)} async-done(((bf16[128,2,128,128]{3,2,1,0:T(8,128)(2,1)}), bf16[128,2,128,128]{3,2,1,0:T(8,128)(2,1)}, u32[]{:S(2)}, u32[]{:S(2)}) %all-to-all-start.1) | async-done | bytes 8388640 | tf_op jit(solution)/shard_map/all_to_all | solution.py:26
  167.8 18.5 %while.46 = (s32[]{:T(128)}, f32[32,128,128]{2,0,1:T(8,128)}, f32[32,128,128]{2,0,1:T(8,128)}, s32[]{:T(128)}, s32[64]{0:T(128)S(1)}, /*index=5*/s32[64,128,128]...) while((s32[]{:T(128)}, f32[32,128,128]{2,0,1:T(8,128)}, ...), condition=%wide.region_5.7_spmd.clone, body=%wide.region_4.6_spmd.clone.sunk | while | flops 812125440 | bytes 44048128 | solution.py:79
  174.2 6.1 fusion.187
  180.7 5.6 fusion.189
  189.7 4.7 copy.165
  206.5 119.0 %all-reduce.12.cloned.1.call-done = (f32[4096,128]{0,1:T(8,128)}, f32[4096,128]{0,1:T(8,128)}) async-done(((f32[4096,128]{0,1:T(8,128)}, f32[4096,128]{0,1:T(8,128)}), (f32[4096,128]{0,1:T(8,128)}, f32[4096,128]{0,1:T(8,128)})) %all-reduce.12.cloned.1.call-update) | async-done | bytes 4194320 | tf_op jit(solution)/shard_map/psum | solution.py:92
  325.5 7.0 fusion.133
  335.4 12.0 %while.47 = (s32[]{:T(128)}, f32[32,128,128]{2,0,1:T(8,128)}, s32[]{:T(128)}, s32[64]{0:T(128)S(1)}, s32[64,128,128]{2,1,0:T(8,128)}, /*index=5*/bf16[32,128,128...) while((s32[]{:T(128)}, f32[32,128,128]{2,0,1:T(8,128)}, ...), condition=%wide.region_11.13_spmd.clone, body=%wide.region_10.12_spmd.clone.sunk | while | flops 472910112 | bytes 15735391 | solution.py:79
  341.6 5.9 fusion.196
  355.9 102.4 %all-reduce.6.cloned.1.call-done = f32[4096,128]{0,1:T(8,128)} async-done(((f32[4096,128]{0,1:T(8,128)}), f32[4096,128]{0,1:T(8,128)}) %all-reduce.6.cloned.1.call-update) | async-done | bytes 2097168 | tf_op jit(solution)/shard_map/psum | solution.py:101
  458.3 5.5 multiply_reduce_fusion.3
  469.1 12.1 %while.48 = (s32[]{:T(128)}, f32[32,128,128]{2,0,1:T(8,128)}, s32[]{:T(128)}, s32[64]{0:T(128)S(1)}, s32[64,128,128]{2,1,0:T(8,128)}, /*index=5*/bf16[32,128,128...) while((s32[]{:T(128)}, f32[32,128,128]{2,0,1:T(8,128)}, ...), condition=%wide.region_16.18_spmd.clone, body=%wide.region_15.17_spmd.clone.sunk | while | flops 472910112 | bytes 15735391 | solution.py:79
  475.3 5.9 fusion.203
  489.5 102.5 %all-reduce.8.cloned.1.call-done = f32[4096,128]{0,1:T(8,128)} async-done(((f32[4096,128]{0,1:T(8,128)}), f32[4096,128]{0,1:T(8,128)}) %all-reduce.8.cloned.1.call-update) | async-done | bytes 2097168 | tf_op jit(solution)/shard_map/psum | solution.py:101
  592.0 5.3 multiply_reduce_fusion.1
  603.7 12.3 %while.49 = (s32[]{:T(128)}, f32[32,128,128]{2,0,1:T(8,128)}, s32[]{:T(128)}, s32[64]{0:T(128)S(1)}, s32[64,128,128]{2,1,0:T(8,128)}, /*index=5*/bf16[32,128,128...) while((s32[]{:T(128)}, f32[32,128,128]{2,0,1:T(8,128)}, ...), condition=%wide.region_21.23_spmd.clone, body=%wide.region_20.22_spmd.clone.sunk | while | flops 472910112 | bytes 15735391 | solution.py:79
  609.9 5.9 fusion.210
  621.9 102.5 %all-reduce.10.cloned.1.call-done = f32[4096,128]{0,1:T(8,128)} async-done(((f32[4096,128]{0,1:T(8,128)}), f32[4096,128]{0,1:T(8,128)}) %all-reduce.10.cloned.1.call-update) | async-done | bytes 2097168 | tf_op jit(solution)/shard_map/psum | solution.py:101
  724.4 5.2 fusion.123
  (105 shorter events, 102.3 us)
Async XLA Ops:
  6.5 21.5 %copy-start = (bf16[4096,128]{1,0:T(8,128)(2,1)S(1)}, bf16[4096,128]{1,0:T(8,128)(2,1)}, u32[]{:S(2)}) copy-start(bf16[4096,128]{1,0:T(8,128)(2,1)} %param.16) | copy-start | bytes 3145732
  6.5 54.0 %all-gather.4.cloned.1.call-start = ((), (), s32[]{:S(2)}) async-start(), calls=%async_computation.2 | async-start | bytes 2228224 | tf_op jit(solution)/shard_map/all_gather | solution.py:88
  8.3 3.5 copy-start.8
  16.8 20.7 %all-to-all-start = ((s32[128,1,2]{2,1,0:T(1,128)}), s32[128,1,2]{2,1,0:T(1,128)S(1)}, u32[]{:S(2)}, u32[]{:S(2)}) async-start(s32[128,1,2]{2,1,0:T(1,128)} %copy.108), calls=%async_computation | async-start | bytes 131072 | tf_op jit(solution)/shard_map/all_to_all | solution.py:22
  28.0 174.7 %all-gather.6.cloned.1.call-start = ((), (), s32[]{:S(2)}) async-start(), calls=%async_computation.6 | async-start | bytes 8454144 | tf_op jit(solution)/shard_map/all_gather | solution.py:42
  53.9 106.3 %all-to-all-start.1 = ((bf16[128,2,128,128]{3,2,1,0:T(8,128)(2,1)}), bf16[128,2,128,128]{3,2,1,0:T(8,128)(2,1)}, u32[]{:S(2)}, u32[]{:S(2)}) async-start(bf16[128,2,128,128]{3,2,1,0:T(8,128)(2,1)} %select_select_fusion), calls=%async_computation.1 | async-start | bytes 16777216 | tf_op jit(solution)/shard_map/all_to_all | solution.py:26
  59.9 265.6 %all-reduce.12.cloned.1.call-start = ((), (), s32[]{:S(2)}) async-start(), calls=%async_computation.7 | async-start | bytes 8388608 | tf_op jit(solution)/shard_map/psum | solution.py:92
  164.6 3.2 copy-start.7
  174.2 6.1 copy-start.2
  202.4 255.9 %all-reduce.6.cloned.1.call-start = ((), (), s32[]{:S(2)}) async-start(), calls=%async_computation.3 | async-start | bytes 4194304 | tf_op jit(solution)/shard_map/psum | solution.py:101
  355.4 236.5 %all-reduce.8.cloned.1.call-start = ((), (), s32[]{:S(2)}) async-start(), calls=%async_computation.4 | async-start | bytes 4194304 | tf_op jit(solution)/shard_map/psum | solution.py:101
  458.3 5.5 copy-start.3
  464.2 2.0 copy-start.4
  489.3 235.1 %all-reduce.10.cloned.1.call-start = ((), (), s32[]{:S(2)}) async-start(), calls=%async_computation.5 | async-start | bytes 4194304 | tf_op jit(solution)/shard_map/psum | solution.py:101
  592.0 5.4 copy-start.5
  597.4 1.6 copy-start.6
  724.4 7.2 copy-start.1
Sparse Core Ops, SparseCore 0:
  9.4 49.4 all-gather.3
  62.1 130.2 all-gather.5
  202.5 122.9 all-reduce.11
  355.5 102.6 all-reduce.5
  489.4 102.5 all-reduce.7
  621.8 102.5 all-reduce.9
